TPU v7x, 32 devices: a whole 2x2x4 slice. The times are simulated.
32 devices in a mesh: grp: 2 (over y), ti: 4 (over x, core), tj: 4 (over z).
Axes of the slice: x: 2, y: 2, z: 4, core: 2. Of those that a mesh axis runs over, the one named last changes fastest.
Arguments:
- corpus: bfloat16 [2, 24576, 1024], P('grp', ('ti', 'tj')), may hold values from -64 to 64
- slot_of_row: int32 [2, 24576], P('grp', ('ti', 'tj')), may hold values from -1 to 24575, as said below
Outputs:
- max_similarity: float32 [2, 12288], P('grp', ('ti', 'tj'))
Inputs may be any that keep to these rules, and one draw needn't show every extreme that they name: `slot_of_row`: every value from 0 to 24575 appears exactly once; a row with value v lies on a device whose ti index is (v % 12288) // 3072; from one device at most 192 rows have values in one aligned group of 768 consecutive values, and some device sends exactly 192 to some group.
All inputs are finite; a program needn't handle non-finite values.
Results may differ from a plain program's by a relative error of at most 0.0009.
Values may be sent and summed in bfloat16 or wider, within the bound.
A program may use at most 64 MiB of HBM per device.

v0:
```python
import jax
import jax.numpy as jnp
from jax import lax
from jax.sharding import PartitionSpec as P

BLK = 3072
epsilon = 1e-06


def per_device(corpus, slot_of_row):
    rows_in = corpus[0]
    values = slot_of_row[0]
    src_count = values.shape[0]
    features = rows_in.shape[1]
    lane_count = lax.axis_size("tj")
    sub_rows = src_count // 2
    cluster = BLK * lax.axis_size("ti")
    capacity = BLK // (lane_count * lane_count)
    owners = 2 * lane_count
    member = values >= 0
    inside = values % cluster
    grid_of = values // cluster
    sub_index = inside % BLK // sub_rows
    owner_of = jnp.where(member, grid_of * lane_count + sub_index, owners)
    onehot = (owner_of[:, None] == jnp.arange(owners, dtype=jnp.int32)[None, :]).astype(jnp.int32)
    rank_in = jnp.sum((jnp.cumsum(onehot, axis=0) - onehot) * onehot, axis=1)
    slot_pos = jnp.where(member, owner_of * capacity + rank_in, owners * capacity)
    send_rows = (
        jnp.zeros((owners * capacity, features), rows_in.dtype)
        .at[slot_pos]
        .set(rows_in, mode="drop")
    )
    send_ids = (
        jnp.full((owners * capacity,), sub_rows, jnp.int32)
        .at[slot_pos]
        .set(inside % sub_rows, mode="drop")
    )
    got_rows, got_ids = (
        lax.all_to_all(
            send_rows.reshape(owners, capacity, features),
            ("grp", "tj"),
            split_axis=0,
            concat_axis=0,
            tiled=True,
        ),
        lax.all_to_all(
            send_ids.reshape(owners, capacity),
            ("grp", "tj"),
            split_axis=0,
            concat_axis=0,
            tiled=True,
        ),
    )
    arrived = (
        jnp.zeros((sub_rows, features), rows_in.dtype)
        .at[got_ids.reshape(-1)]
        .set(got_rows.reshape(-1, features), mode="drop")
    )
    widened = arrived.astype(jnp.float32)
    row_squares = jnp.sum(widened * widened, axis=1, keepdims=True)
    inverse_norm = lax.rsqrt(row_squares + epsilon)
    unit_rows = (widened * inverse_norm).astype(jnp.bfloat16)
    tile_row = lax.axis_index("ti")
    tile_col = lax.axis_index("tj")
    block_rows = lax.all_gather(unit_rows, "tj", axis=0, tiled=True)
    row_slot = tile_row * BLK + jnp.arange(BLK, dtype=jnp.int32)
    portion = lax.all_gather(unit_rows, "ti", axis=0, tiled=True)
    length = portion.shape[0]
    position = jnp.arange(length, dtype=jnp.int32)
    col_slot = position // sub_rows * BLK + tile_col * sub_rows + position % sub_rows
    scores = lax.dot_general(
        block_rows, portion, (((1,), (1,)), ((), ())), preferred_element_type=jnp.float32
    )
    scores = jnp.where(row_slot[:, None] == col_slot[None, :], -2.0, scores)
    tile_best = jnp.maximum(jnp.full((BLK,), -2.0, jnp.float32), jnp.max(scores, axis=1))
    combined = lax.pmax(tile_best, "tj")
    result = lax.dynamic_slice_in_dim(combined, tile_col * sub_rows, sub_rows, 0)
    return result[None, :]


def solution(mesh):
    in_specs = (P("grp", ("ti", "tj"), None), P("grp", ("ti", "tj")))
    out_specs = P("grp", ("ti", "tj"))
    return jax.shard_map(
        per_device, mesh=mesh, in_specs=in_specs, out_specs=out_specs, check_vma=False
    )
```

profile of v0, /device:TPU:0, one launch (start us, length us, event | category | flops | bytes accessed | tf_op | source)
XLA Modules:
  0.0 336.0 jit_solution(1104900848834688039)
XLA Ops:
  6.5 0.0 copy-start
  6.5 0.9 fusion.39
  7.4 0.8 compare_reduce_fusion.1
  8.3 2.3 reduce-window.6
  10.6 0.3 slice_reduce_fusion
  10.9 0.2 reduce-window.9
  11.1 0.1 add_bitcast_fusion
  11.2 0.8 fusion.32
  12.0 6.2 %scatter_custom_fusion = s32[1536]{0:T(1024)S(1)} fusion(s32[1536]{0:T(1024)S(1)} %fusion.32, s32[1536]{0:T(1024)S(1)} %get-tuple-element.9, s32[]{:T(128)} %constant.74.clone.1), kind=kCustom, calls=%fused_computation.82 | custom fusion | bytes 6148 | tf_op jit(solution)/shard_map/scatter | solution.py:36
  18.2 0.7 all_to_all.9
  18.9 7.3 %all-to-all-start = ((s32[8,1,192]{2,1,0:T(1,128)}), s32[8,1,192]{2,1,0:T(1,128)S(1)}, u32[]{:S(2)}, u32[]{:S(2)}) async-start(s32[8,1,192]{2,1,0:T(1,128)} %all_to_all.9), calls=%async_computation | async-start | bytes 16384 | tf_op jit(solution)/shard_map/all_to_all | solution.py:46
  26.2 0.0 copy-done
  26.2 9.7 %scatter_custom_fusion.1 = bf16[1536,1024]{1,0:T(8,128)(2,1)} fusion(s32[1536]{0:T(1024)S(1)} %fusion.32, bf16[1,1536,1024]{2,1,0:T(8,128)(2,1)S(1)} %copy-done, bf16[]{:T(256)} %constant.78.clone.1), kind=kCustom, calls=%fused_computation.8 | custom fusion | bytes 6291458 | tf_op jit(solution)/shard_map/scatter | solution.py:31
  35.9 0.0 all-to-all-done
  35.9 6.0 %all-to-all-start.1 = ((bf16[8,192,1024]{2,1,0:T(8,128)(2,1)}), bf16[8,192,1024]{2,1,0:T(8,128)(2,1)}, u32[]{:S(2)}, u32[]{:S(2)}) async-start(bf16[8,192,1024]{2,1,0:T(8,128)(2,1)} %bitcast.80), calls=%async_computation.1 | async-start | bytes 6291456 | tf_op jit(solution)/shard_map/all_to_all | solution.py:39
  41.9 0.0 all-gather.3.cloned.1.call-start
  42.0 0.1 reshape.266
  42.1 70.9 %all-to-all-done.1 = bf16[8,192,1024]{2,1,0:T(8,128)(2,1)} async-done(((bf16[8,192,1024]{2,1,0:T(8,128)(2,1)}), bf16[8,192,1024]{2,1,0:T(8,128)(2,1)}, u32[]{:S(2)}, u32[]{:S(2)}) %all-to-all-start.1) | async-done | bytes 3145760 | tf_op jit(solution)/shard_map/all_to_all | solution.py:39
  113.0 9.5 %scatter_custom_fusion.2 = bf16[768,1024]{1,0:T(8,128)(2,1)} fusion(s32[1536]{0:T(1024)S(1)} %fusion.33, bf16[1536,1024]{1,0:T(8,128)(2,1)} %bitcast.7, bf16[]{:T(256)} %constant.78.clone.1), kind=kCustom, calls=%fused_computation.11 | custom fusion | bytes 1573376 | tf_op jit(solution)/shard_map/scatter | solution.py:57
  122.5 1.8 fusion
  124.2 2.9 fusion.1
  127.2 0.0 all-gather.3.cloned.1.call-update
  127.2 0.2 all-gather.5.cloned.1.call-start
  127.4 0.5 all-gather.5.cloned.1.call-update
  128.0 112.0 %all-gather.3.cloned.1.call-done = bf16[3072,1024]{1,0:T(8,128)(2,1)} async-done(((bf16[768,1024]{1,0:T(8,128)(2,1)}), bf16[3072,1024]{1,0:T(8,128)(2,1)}) %all-gather.3.cloned.1.call-update) | async-done | bytes 6291472 | tf_op jit(solution)/shard_map/all_gather | solution.py:65
  240.0 46.1 %all-gather.5.cloned.1.call-done = bf16[3072,1024]{1,0:T(8,128)(2,1)} async-done(((bf16[768,1024]{1,0:T(8,128)(2,1)}), bf16[3072,1024]{1,0:T(8,128)(2,1)}) %all-gather.5.cloned.1.call-update) | async-done | bytes 6291472 | tf_op jit(solution)/shard_map/all_gather | solution.py:67
  286.2 23.7 %select_reduce_fusion = f32[3072]{0:T(1024)S(1)} fusion(bf16[3072,1024]{1,0:T(8,128)(2,1)} %all-gather.3.cloned.1.call-done, bf16[3072,1024]{1,0:T(8,128)(2,1)} %all-gather.5.cloned.1.call-done, s32[3072]{0:T(1024)S(1)} %iota_add_fusion, s32[3072]{0:T(1024)S(1)} %fusion.20), kind=kOutput, calls=%fused_computation.3 | convolution fusion | flops 19355660288 | bytes 12619776 | tf_op jit(solution)/shard_map/dot_general | solution.py:71
  309.8 18.7 %pmax.7 = f32[3072]{0:T(1024)S(1)} all-reduce(f32[3072]{0:T(1024)S(1)} %broadcast_maximum_fusion), channel_id=1, replica_groups=mesh['grp'=2,'ti'=4,'tj'=4] {'tj'}, use_global_device_ids=true, to_apply=%region_8.9 | all-reduce | flops 3072 | bytes 24576 | tf_op jit(solution)/shard_map/pmax | solution.py:76
  328.5 0.1 dynamic_slice.3
  328.6 0.6 broadcast_in_dim.43
  (10 shorter events, 0.2 us)
Async XLA Ops:
  6.5 19.7 %copy-start = (bf16[1,1536,1024]{2,1,0:T(8,128)(2,1)S(1)}, bf16[1,1536,1024]{2,1,0:T(8,128)(2,1)}, u32[]{:S(2)}) copy-start(bf16[1,1536,1024]{2,1,0:T(8,128)(2,1)} %param.2) | copy-start | bytes 9437188
  18.9 17.0 %all-to-all-start = ((s32[8,1,192]{2,1,0:T(1,128)}), s32[8,1,192]{2,1,0:T(1,128)S(1)}, u32[]{:S(2)}, u32[]{:S(2)}) async-start(s32[8,1,192]{2,1,0:T(1,128)} %all_to_all.9), calls=%async_computation | async-start | bytes 16384 | tf_op jit(solution)/shard_map/all_to_all | solution.py:46
  35.9 77.1 %all-to-all-start.1 = ((bf16[8,192,1024]{2,1,0:T(8,128)(2,1)}), bf16[8,192,1024]{2,1,0:T(8,128)(2,1)}, u32[]{:S(2)}, u32[]{:S(2)}) async-start(bf16[8,192,1024]{2,1,0:T(8,128)(2,1)} %bitcast.80), calls=%async_computation.1 | async-start | bytes 6291456 | tf_op jit(solution)/shard_map/all_to_all | solution.py:39
  41.9 198.1 %all-gather.3.cloned.1.call-start = ((), (), s32[]{:S(2)}) async-start(), calls=%async_computation.2 | async-start | bytes 7864320 | tf_op jit(solution)/shard_map/all_gather | solution.py:65
  127.2 159.0 %all-gather.5.cloned.1.call-start = ((), (), s32[]{:S(2)}) async-start(), calls=%async_computation.3 | async-start | bytes 7864320 | tf_op jit(solution)/shard_map/all_gather | solution.py:67
Sparse Core Ops, SparseCore 0:
  127.3 112.6 all-gather.2
  241.6 44.5 all-gather.4
where the time goes:
time: 336 us
  waiting for transfers between devices  230 us (68%)
  local copies, waits for them, and re-layouts  27 us (8%)
  matrix products  23.7 us (7%)
  blocking collectives  18.7 us (6%)
  starting transfers between devices  13.6 us (4%)
  between operations  13.5 us (4%)
  other arithmetic  9.96 us (3%)
    all_gather x1, waiting for transfers between devices, per_device(): block_rows = lax.all_gather(unit_rows, 'tj', axis=0, tiled=True)  112 us
    all_to_all x1, waiting for transfers between devices, per_device(): lax.all_to_all(send_rows.reshape(owners, capacity, features), ('grp', 'tj...  70.9 us
    all_gather x1, waiting for transfers between devices, per_device(): portion = lax.all_gather(unit_rows, 'ti', axis=0, tiled=True)  46.1 us
    dot_general x1, matrix products, per_device(): lax.dot_general(block_rows, portion, (((1,), (1,)), ((), ())), preferred_...  23.7 us
    pmax x1, blocking collectives, per_device(): combined = lax.pmax(tile_best, 'tj')  18.7 us
    scatter x1, local copies, waits for them, and re-layouts, per_device(): send_rows = jnp.zeros((owners * capacity, features), rows_in.dtype).at[sl...  9.66 us
    scatter x1, local copies, waits for them, and re-layouts, per_device(): arrived = jnp.zeros((sub_rows, features), rows_in.dtype).at[got_ids.resha...  9.47 us
    all_to_all x1, starting transfers between devices, per_device(): lax.all_to_all(send_ids.reshape(owners, capacity), ('grp', 'tj'), split_a...  7.31 us
  transfers between devices with their start and end apart: 4, of which 3 were waited for; matrix products, arithmetic and copies ran while one was open for 3% of the time, Pallas kernels for 0%

commit v1 on v0

--- a/solution.py
+++ b/solution.py
@@ -64,7 +64,12 @@
     tile_col = lax.axis_index("tj")
     block_rows = lax.all_gather(unit_rows, "tj", axis=0, tiled=True)
     row_slot = tile_row * BLK + jnp.arange(BLK, dtype=jnp.int32)
-    portion = lax.all_gather(unit_rows, "ti", axis=0, tiled=True)
+    ring = [unit_rows]
+    for hop in range(3):
+        ring.append(lax.ppermute(ring[-1], "ti", [(dev, (dev + 1) % 4) for dev in range(4)]))
+    portion = jnp.roll(
+        jnp.concatenate(ring[::-1], axis=0), (lax.axis_index("ti") + 1) * ring[0].shape[0], axis=0
+    )
     length = portion.shape[0]
     position = jnp.arange(length, dtype=jnp.int32)
     col_slot = position // sub_rows * BLK + tile_col * sub_rows + position % sub_rows

time: 336 us -> 287 us (0.85)
  waiting for transfers between devices: 230 us -> 166 us
  local copies, waits for them, and re-layouts: 27 us -> 41.7 us
    all_gather x1, waiting for transfers between devices: 112 us -> 34.9 us  [per_device(): block_rows = lax.all_gather(unit_rows, 'tj', axis=0, tiled=True)]
    ppermute x0 -> x3, waiting for transfers between devices: none -> 60.1 us  [per_device(): lax.ppermute(ring[-1], 'ti', [(dev, (dev + 1) % 4) for dev in range(4)])]
    all_gather x1 -> x0, waiting for transfers between devices: 46.1 us -> none  [per_device(): portion = lax.all_gather(unit_rows, 'ti', axis=0, tiled=True)]
    unnamed x2 -> x14, local copies, waits for them, and re-layouts: 0.01 us -> 14.7 us
  transfers between devices with their start and end apart: 4 -> 6, of which waited for: 3 -> 5; matrix products, arithmetic and copies ran while one was open for 3% -> 9% of each run, Pallas kernels for 0% -> 0%
where the time goes in v1:
time: 287 us
  waiting for transfers between devices  166 us (58%)
  local copies, waits for them, and re-layouts  41.7 us (15%)
  matrix products  23.8 us (8%)
  blocking collectives  15.7 us (5%)
  between operations  13.5 us (5%)
  starting transfers between devices  13.4 us (5%)
  other arithmetic  12.9 us (4%)
    all_to_all x1, waiting for transfers between devices, per_device(): lax.all_to_all(send_rows.reshape(owners, capacity, features), ('grp', 'tj...  70.9 us
    ppermute x3, waiting for transfers between devices, per_device(): lax.ppermute(ring[-1], 'ti', [(dev, (dev + 1) % 4) for dev in range(4)])  60.1 us
    all_gather x1, waiting for transfers between devices, per_device(): block_rows = lax.all_gather(unit_rows, 'tj', axis=0, tiled=True)  34.9 us
    dot_general x1, matrix products, per_device(): lax.dot_general(block_rows, portion, (((1,), (1,)), ((), ())), preferred_...  23.8 us
    pmax x1, blocking collectives, per_device(): combined = lax.pmax(tile_best, 'tj')  15.7 us
    unnamed x14, local copies, waits for them, and re-layouts  14.7 us
    scatter x1, local copies, waits for them, and re-layouts, per_device(): send_rows = jnp.zeros((owners * capacity, features), rows_in.dtype).at[sl...  9.66 us
    scatter x1, local copies, waits for them, and re-layouts, per_device(): arrived = jnp.zeros((sub_rows, features), rows_in.dtype).at[got_ids.resha...  9.48 us
  transfers between devices with their start and end apart: 6, of which 5 were waited for; matrix products, arithmetic and copies ran while one was open for 9% of the time, Pallas kernels for 0%

profile of v1, /device:TPU:0, one launch (start us, length us, event | category | flops | bytes accessed | tf_op | source)
XLA Modules:
  0.0 287.0 jit_solution(15109673049695555482)
XLA Ops:
  6.5 0.0 copy-start
  6.5 0.9 fusion.41
  7.4 0.8 compare_reduce_fusion.1
  8.3 2.3 reduce-window.6
  10.6 0.3 slice_reduce_fusion
  10.9 0.2 reduce-window.9
  11.1 0.1 add_bitcast_fusion
  11.2 0.8 fusion.33
  12.0 6.2 %scatter_custom_fusion = s32[1536]{0:T(1024)S(1)} fusion(s32[1536]{0:T(1024)S(1)} %fusion.33, s32[1536]{0:T(1024)S(1)} %get-tuple-element.9, s32[]{:T(128)} %constant.88.clone.1), kind=kCustom, calls=%fused_computation.91 | custom fusion | bytes 6148 | tf_op jit(solution)/shard_map/scatter | solution.py:36
  18.2 0.7 all_to_all.9
  18.9 7.3 %all-to-all-start = ((s32[8,1,192]{2,1,0:T(1,128)}), s32[8,1,192]{2,1,0:T(1,128)S(1)}, u32[]{:S(2)}, u32[]{:S(2)}) async-start(s32[8,1,192]{2,1,0:T(1,128)} %all_to_all.9), calls=%async_computation | async-start | bytes 16384 | tf_op jit(solution)/shard_map/all_to_all | solution.py:46
  26.2 0.0 copy-done
  26.2 9.7 %scatter_custom_fusion.1 = bf16[1536,1024]{1,0:T(8,128)(2,1)} fusion(s32[1536]{0:T(1024)S(1)} %fusion.33, bf16[1,1536,1024]{2,1,0:T(8,128)(2,1)S(1)} %copy-done, bf16[]{:T(256)} %constant.92.clone.1), kind=kCustom, calls=%fused_computation.9 | custom fusion | bytes 6291458 | tf_op jit(solution)/shard_map/scatter | solution.py:31
  35.9 0.0 all-to-all-done
  35.9 6.0 %all-to-all-start.1 = ((bf16[8,192,1024]{2,1,0:T(8,128)(2,1)}), bf16[8,192,1024]{2,1,0:T(8,128)(2,1)}, u32[]{:S(2)}, u32[]{:S(2)}) async-start(bf16[8,192,1024]{2,1,0:T(8,128)(2,1)} %bitcast.79), calls=%async_computation.1 | async-start | bytes 6291456 | tf_op jit(solution)/shard_map/all_to_all | solution.py:39
  41.9 0.0 all-gather.2.cloned.1.call-start
  42.0 0.1 reshape.266
  42.1 70.9 %all-to-all-done.1 = bf16[8,192,1024]{2,1,0:T(8,128)(2,1)} async-done(((bf16[8,192,1024]{2,1,0:T(8,128)(2,1)}), bf16[8,192,1024]{2,1,0:T(8,128)(2,1)}, u32[]{:S(2)}, u32[]{:S(2)}) %all-to-all-start.1) | async-done | bytes 3145760 | tf_op jit(solution)/shard_map/all_to_all | solution.py:39
  113.0 9.5 %scatter_custom_fusion.2 = bf16[768,1024]{1,0:T(8,128)(2,1)} fusion(s32[1536]{0:T(1024)S(1)} %fusion.34, bf16[1536,1024]{1,0:T(8,128)(2,1)} %bitcast.7, bf16[]{:T(256)} %constant.92.clone.1), kind=kCustom, calls=%fused_computation.12 | custom fusion | bytes 1573376 | tf_op jit(solution)/shard_map/scatter | solution.py:57
  122.5 1.8 fusion.1
  124.3 2.9 %fusion.2 = bf16[768,1024]{1,0:T(8,128)(2,1)} fusion(bf16[768,1024]{1,0:T(8,128)(2,1)} %scatter_custom_fusion.2, f32[768]{0:T(1024)S(1)} %add_rsqrt_fusion), kind=kLoop, calls=%fused_computation.8 | loop fusion | flops 2359296 | bytes 3148800 | tf_op jit(solution)/shard_map/convert_element_type | solution.py:62
  127.1 0.0 all-gather.2.cloned.1.call-update
  127.2 0.1 collective-permute-start
  127.2 20.0 %collective-permute-done = bf16[768,1024]{1,0:T(8,128)(2,1)S(1)} collective-permute-done((bf16[768,1024]{1,0:T(8,128)(2,1)}, bf16[768,1024]{1,0:T(8,128)(2,1)S(1)}, u32[]{:S(2)}, u32[]{:S(2)}) %collective-permute-start) | collective-permute-done | bytes 1572896 | tf_op jit(solution)/shard_map/ppermute | solution.py:69
  147.3 0.0 copy-start.2
  147.3 1.2 copy-done.2
  148.5 0.0 collective-permute-start.1
  148.5 19.9 %collective-permute-done.1 = bf16[768,1024]{1,0:T(8,128)(2,1)} collective-permute-done((bf16[768,1024]{1,0:T(8,128)(2,1)S(1)}, bf16[768,1024]{1,0:T(8,128)(2,1)}, u32[]{:S(2)}, u32[]{:S(2)}) %collective-permute-start.1) | collective-permute-done | bytes 1572896 | tf_op jit(solution)/shard_map/ppermute | solution.py:69
  168.5 0.0 collective-permute-start.2
  168.5 0.0 copy-start.3
  168.5 20.1 %collective-permute-done.2 = bf16[768,1024]{1,0:T(8,128)(2,1)} collective-permute-done((bf16[768,1024]{1,0:T(8,128)(2,1)}, bf16[768,1024]{1,0:T(8,128)(2,1)}, u32[]{:S(2)}, u32[]{:S(2)}) %collective-permute-start.2) | collective-permute-done | bytes 1572896 | tf_op jit(solution)/shard_map/ppermute | solution.py:69
  188.6 2.7 constant_dynamic-update-slice_fusion.7
  191.3 0.0 copy-start.1
  191.3 2.8 constant_dynamic-update-slice_fusion.6
  194.1 0.0 copy-done.3
  194.1 1.3 constant_dynamic-update-slice_fusion.5
  195.4 0.0 copy-done.1
  195.4 1.5 constant_dynamic-update-slice_fusion.4
  196.9 2.7 constant_dynamic-update-slice_fusion.3
  199.5 2.8 constant_dynamic-update-slice_fusion.2
  202.3 1.3 constant_dynamic-update-slice_fusion.1
  203.6 1.5 constant_dynamic-update-slice_fusion
  205.0 34.9 %all-gather.2.cloned.1.call-done = bf16[3072,1024]{1,0:T(8,128)(2,1)} async-done(((bf16[768,1024]{1,0:T(8,128)(2,1)}), bf16[3072,1024]{1,0:T(8,128)(2,1)}) %all-gather.2.cloned.1.call-update) | async-done | bytes 6291472 | tf_op jit(solution)/shard_map/all_gather | solution.py:65
  240.0 23.8 %select_reduce_fusion = f32[3072]{0:T(1024)S(1)} fusion(bf16[3072,1024]{1,0:T(8,128)(2,1)} %all-gather.2.cloned.1.call-done, s32[3072]{0:T(1024)S(1)} %iota_add_fusion, s32[3072]{0:T(1024)S(1)} %fusion.21, bf16[6144,1024]{1,0:T(8,128)(2,1)} %constant_dynamic-update-slice_fusion, s32[]{:T(128)S(6)} %select_n.193), kind=kOutput, calls=%fused_computation.3 | convolution fusion | flops 19355660288 | bytes 12619780 | tf_op jit(solution)/shard_map/dot_general | solution.py:76
  263.8 15.7 %pmax.7 = f32[3072]{0:T(1024)S(1)} all-reduce(f32[3072]{0:T(1024)S(1)} %broadcast_maximum_fusion), channel_id=1, replica_groups=mesh['grp'=2,'ti'=4,'tj'=4] {'tj'}, use_global_device_ids=true, to_apply=%region_8.9 | all-reduce | flops 3072 | bytes 24576 | tf_op jit(solution)/shard_map/pmax | solution.py:81
  279.5 0.1 dynamic_slice.8
  279.5 0.6 broadcast_in_dim.43
  (10 shorter events, 0.2 us)
Async XLA Ops:
  6.5 19.7 %copy-start = (bf16[1,1536,1024]{2,1,0:T(8,128)(2,1)S(1)}, bf16[1,1536,1024]{2,1,0:T(8,128)(2,1)}, u32[]{:S(2)}) copy-start(bf16[1,1536,1024]{2,1,0:T(8,128)(2,1)} %param.2) | copy-start | bytes 9437188
  18.9 17.0 %all-to-all-start = ((s32[8,1,192]{2,1,0:T(1,128)}), s32[8,1,192]{2,1,0:T(1,128)S(1)}, u32[]{:S(2)}, u32[]{:S(2)}) async-start(s32[8,1,192]{2,1,0:T(1,128)} %all_to_all.9), calls=%async_computation | async-start | bytes 16384 | tf_op jit(solution)/shard_map/all_to_all | solution.py:46
  35.9 77.1 %all-to-all-start.1 = ((bf16[8,192,1024]{2,1,0:T(8,128)(2,1)}), bf16[8,192,1024]{2,1,0:T(8,128)(2,1)}, u32[]{:S(2)}, u32[]{:S(2)}) async-start(bf16[8,192,1024]{2,1,0:T(8,128)(2,1)} %bitcast.79), calls=%async_computation.1 | async-start | bytes 6291456 | tf_op jit(solution)/shard_map/all_to_all | solution.py:39
  41.9 198.1 %all-gather.2.cloned.1.call-start = ((), (), s32[]{:S(2)}) async-start(), calls=%async_computation.2 | async-start | bytes 7864320 | tf_op jit(solution)/shard_map/all_gather | solution.py:65
  127.2 20.1 %collective-permute-start = (bf16[768,1024]{1,0:T(8,128)(2,1)}, bf16[768,1024]{1,0:T(8,128)(2,1)S(1)}, u32[]{:S(2)}, u32[]{:S(2)}) collective-permute-start(bf16[768,1024]{1,0:T(8,128)(2,1)} %fusion.2), channel_id=1, source_target_pairs={{0,4},{4,8},{8,12},{12,0},{1,5},{5,9},{9,13},{13,1},{2,6},{6,10},{... | collective-permute-start | bytes 4718600 | tf_op jit(solution)/shard_map/ppermute | solution.py:69
  147.3 1.2 copy-start.2
  148.5 19.9 %collective-permute-start.1 = (bf16[768,1024]{1,0:T(8,128)(2,1)S(1)}, bf16[768,1024]{1,0:T(8,128)(2,1)}, u32[]{:S(2)}, u32[]{:S(2)}) collective-permute-start(bf16[768,1024]{1,0:T(8,128)(2,1)S(1)} %collective-permute-done), channel_id=1, source_target_pairs={{0,4},{4,8},{8,12},{12,0},{1,5},{5,9},{9,13},{13,1},{2,6},{6,10},{... | collective-permute-start | bytes 4718600 | tf_op jit(solution)/shard_map/ppermute | solution.py:69
  168.5 20.2 %collective-permute-start.2 = (bf16[768,1024]{1,0:T(8,128)(2,1)}, bf16[768,1024]{1,0:T(8,128)(2,1)}, u32[]{:S(2)}, u32[]{:S(2)}) collective-permute-start(bf16[768,1024]{1,0:T(8,128)(2,1)} %collective-permute-done.1), channel_id=1, source_target_pairs={{0,4},{4,8},{8,12},{12,0},{1,5},{5,9},{9,13},{13,1},{2,6},{6,10},{... | collective-permute-start | bytes 4718600 | tf_op jit(solution)/shard_map/ppermute | solution.py:69
  168.5 25.6 %copy-start.3 = (bf16[768,1024]{1,0:T(8,128)(2,1)S(1)}, bf16[768,1024]{1,0:T(8,128)(2,1)}, u32[]{:S(2)}) copy-start(bf16[768,1024]{1,0:T(8,128)(2,1)} %copy-done.2) | copy-start | bytes 4718596
  191.3 4.1 %copy-start.1 = (bf16[768,1024]{1,0:T(8,128)(2,1)S(1)}, bf16[768,1024]{1,0:T(8,128)(2,1)}, u32[]{:S(2)}) copy-start(bf16[768,1024]{1,0:T(8,128)(2,1)} %scatter_custom_fusion.2) | copy-start | bytes 4718596
Sparse Core Ops, SparseCore 0:
  127.3 112.6 all-gather.1
